TPU v7x, 128 devices: a whole 4x4x4 slice. The times are simulated.
128 devices in a mesh: seq: 8 (over y, core), vocab: 16 (over x, z).
Axes of the slice: x: 4, y: 4, z: 4, core: 2. Of those that a mesh axis runs over, the one named last changes fastest.
Arguments:
- queries: bfloat16 [8192, 2, 2048], P(('seq', 'vocab')), may hold values from -40 to 40
- key_vectors: bfloat16 [8192, 2, 2048], P(('seq', 'vocab')), may hold values from -40 to 40
- value_vectors: bfloat16 [8192, 2, 2048], P(('seq', 'vocab')), may hold values from -18 to 18
- residual: bfloat16 [8192, 2, 2048], P(('seq', 'vocab')), may hold values from -3 to 3
- norm_gain: float32 [2048], replicated, may hold values from 0.1 to 1.9
- head_weight: bfloat16 [2048, 16384], P(None, 'vocab'), may hold values from -0.125 to 0.125
- head_bias: float32 [16384], P('vocab'), may hold values from -6 to 6
- doc_lengths: int32 [2], replicated, may hold values from 1 to 8192, 12288 in all
Outputs:
- pooled: float32 [2, 16384], P(None, 'vocab')
- grad_hidden: bfloat16 [8192, 2, 2048], P(('seq', 'vocab'))
Inputs may be any that keep to these rules, and one draw needn't show every extreme that they name: `doc_lengths`: the lengths add up to 12288.
All inputs are finite; a program needn't handle non-finite values.
Results may differ from a plain program's by a relative error of at most 0.018.
Values may be sent and summed in bfloat16 or wider, within the bound.
No kernel may reach another device: no remote copies, remote signals or barrier semaphores. Data moves between devices by JAX's collectives and lax.ppermute only.
A program may use at most 128 MiB of HBM per device.

v0:
```python
import math
import jax
import jax.numpy as jnp
from jax import lax
from jax.sharding import PartitionSpec as P

HEAD_DIM = 128
sharpness = 8.0
flops_weight = 500.0
epsilon = 1e-05


def local(
    queries, key_vectors, value_vectors, residual, norm_gain, head_weight, head_bias, doc_lengths
):
    tokens_here = queries.shape[0]
    docs_count = queries.shape[1]
    vocab_count = lax.axis_size("vocab")
    seq_at = lax.axis_index("seq")
    query_heads, key_heads, value_heads = (
        lax.all_to_all(queries, "seq", split_axis=2, concat_axis=0, tiled=True),
        lax.all_to_all(key_vectors, "seq", split_axis=2, concat_axis=0, tiled=True),
        lax.all_to_all(value_vectors, "seq", split_axis=2, concat_axis=0, tiled=True),
    )
    block_rows = query_heads.shape[0]
    local_width = query_heads.shape[2]
    local_heads = local_width // HEAD_DIM
    query_split = query_heads.reshape(block_rows, docs_count, local_heads, HEAD_DIM)
    within = jnp.arange(block_rows, dtype=jnp.int32)

    def attend_block(carry, block):
        highest, total, summed = carry
        key_block, value_block, shard = block
        key_split = key_block.reshape(block_rows, docs_count, local_heads, HEAD_DIM)
        value_split = value_block.reshape(block_rows, docs_count, local_heads, HEAD_DIM)
        key_place = (
            within // tokens_here * vocab_count + shard
        ) * tokens_here + within % tokens_here
        allowed = (key_place[None, :] < doc_lengths[:, None])[:, None, None, :]
        scores = jnp.einsum(
            "qbhe,kbhe->bhqk", query_split, key_split, preferred_element_type=jnp.float32
        ) / math.sqrt(HEAD_DIM)
        block_top = jnp.max(jnp.where(allowed, scores, -1e30), axis=3)
        new_top = jnp.maximum(highest, block_top)
        weights = jnp.where(allowed, jnp.exp(scores - new_top[..., None]), 0.0)
        shrink = jnp.exp(highest - new_top)
        total = total * shrink + jnp.sum(weights, axis=3)
        added = jnp.einsum(
            "bhqk,kbhe->qbhe",
            weights.astype(jnp.bfloat16),
            value_split,
            preferred_element_type=jnp.float32,
        )
        summed = summed * jnp.transpose(shrink, (2, 0, 1))[..., None] + added
        return ((new_top, total, summed), None)

    initial = (
        jnp.full((docs_count, local_heads, block_rows), -1e30, jnp.float32),
        jnp.zeros((docs_count, local_heads, block_rows), jnp.float32),
        jnp.zeros((block_rows, docs_count, local_heads, HEAD_DIM), jnp.float32),
    )
    carry = initial
    key_piece = lax.all_gather(key_heads, "vocab", axis=0, tiled=True)
    value_piece = lax.all_gather(value_heads, "vocab", axis=0, tiled=True)
    count = key_piece.shape[0] // block_rows
    key_blocks = key_piece.reshape(count, block_rows, docs_count, local_width)
    value_blocks = value_piece.reshape(count, block_rows, docs_count, local_width)
    shards = jnp.arange(count, dtype=jnp.int32)
    carry, unused = lax.scan(attend_block, carry, (key_blocks, value_blocks, shards))
    highest, total, summed = carry
    attended = (
        (summed / jnp.transpose(total, (2, 0, 1))[..., None])
        .reshape(block_rows, docs_count, local_width)
        .astype(jnp.bfloat16)
    )
    returned = lax.all_to_all(attended, "seq", split_axis=0, concat_axis=2, tiled=True)
    combined = residual.astype(jnp.float32) + returned.astype(jnp.float32)
    inv_rms = lax.rsqrt(jnp.mean(combined * combined, axis=2, keepdims=True) + epsilon)
    hidden = (combined * inv_rms * norm_gain).astype(jnp.bfloat16)
    arrived = lax.all_gather(hidden, "vocab", axis=0, tiled=True)
    row_count = arrived.shape[0]
    flattened = jnp.dot(
        arrived.reshape(row_count * docs_count, arrived.shape[2]),
        head_weight,
        preferred_element_type=jnp.float32,
    )
    logits = flattened.reshape(row_count, docs_count, head_weight.shape[1]) + head_bias
    gathered_rows = logits.shape[0]
    row_index = jnp.arange(gathered_rows, dtype=jnp.int32)
    position = (
        seq_at * vocab_count + row_index // tokens_here
    ) * tokens_here + row_index % tokens_here
    row_allowed = position[:, None] < doc_lengths[None, :]
    saturated = jnp.log1p(jnp.maximum(logits, 0.0))
    boosted = jnp.where(row_allowed[:, :, None], jnp.exp(sharpness * saturated), 0.0)
    partial_sums = jnp.sum(boosted, axis=0)
    lengths_float = doc_lengths[:, None].astype(jnp.float32)
    totals = lax.psum(partial_sums, "seq")
    pooled = jnp.log(totals / lengths_float) / sharpness
    coefficient = 2.0 * flops_weight / docs_count * jnp.mean(pooled, axis=0)[None, :] / totals
    derivative = jnp.where(logits > 0.0, 1.0 / (1.0 + jnp.maximum(logits, 0.0)), 0.0)
    dlogits = (coefficient[None, :, :] * boosted * derivative).astype(jnp.bfloat16)
    flattened = lax.dot_general(
        dlogits.reshape(gathered_rows * docs_count, dlogits.shape[2]),
        head_weight,
        (((1,), (1,)), ((), ())),
        preferred_element_type=jnp.float32,
    )
    own_rows = lax.psum_scatter(
        flattened.reshape(gathered_rows, docs_count, head_weight.shape[0]).astype(jnp.bfloat16),
        "vocab",
        scatter_dimension=0,
        tiled=True,
    )
    return (pooled, own_rows)


def solution(mesh):
    in_specs = (
        P(("seq", "vocab"), None, None),
        P(("seq", "vocab"), None, None),
        P(("seq", "vocab"), None, None),
        P(("seq", "vocab"), None, None),
        P(),
        P(None, "vocab"),
        P("vocab"),
        P(),
    )
    out_specs = (P(None, "vocab"), P(("seq", "vocab"), None, None))
    return jax.shard_map(local, mesh=mesh, in_specs=in_specs, out_specs=out_specs, check_vma=False)
```

profile of v0, /device:TPU:0, one launch (start us, length us, event | category | flops | bytes accessed | tf_op | source)
XLA Modules:
  0.0 576.1 jit_solution(2232000277719809404)
XLA Ops:
  10.6 14.7 %all_to_all.60 = bf16[8,2,16384]{2,1,0:T(2,128)(2,1)S(1)} all-to-all(bf16[8,2,16384]{2,1,0:T(2,128)(2,1)S(1)} %reshape.212), channel_id=1, replica_groups=mesh['seq'=8,'vocab'=16] {'seq'}, dimensions={0} | all-to-all | bytes 1048576 | tf_op jit(solution)/shard_map/all_to_all | solution.py:23
  31.2 12.8 %all_to_all.61 = bf16[8,2,16384]{2,1,0:T(2,128)(2,1)S(1)} all-to-all(bf16[8,2,16384]{2,1,0:T(2,128)(2,1)S(1)} %reshape.208), channel_id=1, replica_groups=mesh['seq'=8,'vocab'=16] {'seq'}, dimensions={0} | all-to-all | bytes 1048576 | tf_op jit(solution)/shard_map/all_to_all | solution.py:22
  49.0 3.5 all-to-all-start.1
  52.6 10.2 %all-to-all-done.1 = bf16[8,2,16384]{2,1,0:T(2,128)(2,1)S(1)} async-done(((bf16[8,2,16384]{2,1,0:T(2,128)(2,1)}), bf16[8,2,16384]{2,1,0:T(2,128)(2,1)S(1)}, u32[]{:S(2)}, u32[]{:S(2)}) %all-to-all-start.1) | async-done | bytes 524320 | tf_op jit(solution)/shard_map/all_to_all | solution.py:21
  64.3 35.0 %all-gather.6.cloned.1.call-done = bf16[8192,2,256]{2,0,1:T(8,128)(2,1)} async-done(((bf16[512,2,256]{2,0,1:T(8,128)(2,1)}), bf16[8192,2,256]{2,0,1:T(8,128)(2,1)}) %all-gather.6.cloned.1.call-update) | async-done | bytes 8388624 | tf_op jit(solution)/shard_map/all_gather | solution.py:64
  99.3 73.3 %all-gather.4.cloned.1.call-done = bf16[8192,2,256]{2,0,1:T(8,128)(2,1)} async-done(((bf16[512,2,256]{2,0,1:T(8,128)(2,1)}), bf16[8192,2,256]{2,0,1:T(8,128)(2,1)}) %all-gather.4.cloned.1.call-update) | async-done | bytes 8388624 | tf_op jit(solution)/shard_map/all_gather | solution.py:63
  172.6 168.6 %while.20 = (s32[]{:T(128)}, f32[2,2,512]{2,1,0:T(2,128)S(1)}, f32[2,2,512]{2,1,0:T(2,128)S(1)}, f32[512,2,2,128]{0,3,2,1:T(8,128)S(1)}, s32[16]{0:T(128)S(1)}, ...) while((s32[]{:T(128)}, f32[2,2,512]{2,1,0:T(2,128)S(1)}, ...), condition=%wide.region_3.4_spmd.clone.clone, body=%wide.region_0.3_spmd.clone.clone.sunk | while | flops 549213184 | bytes 37364912 | solution.py:69
  175.5 3.0 select_reduce_fusion.2
  178.7 3.5 fusion.75
  186.0 3.0 select_reduce_fusion.2
  189.3 3.5 fusion.75
  199.8 3.5 fusion.75
  210.3 3.5 fusion.75
  220.9 3.5 fusion.75
  231.4 3.5 fusion.75
  241.9 3.5 fusion.75
  252.5 3.5 fusion.75
  263.0 3.5 fusion.75
  273.5 3.5 fusion.75
  284.1 3.5 fusion.75
  294.6 3.5 fusion.75
  305.2 3.5 fusion.75
  315.7 3.5 fusion.75
  326.2 3.5 fusion.75
  336.8 3.5 fusion.75
  341.8 14.4 %all_to_all.62 = bf16[512,2,256]{2,1,0:T(2,128)(2,1)S(1)} all-to-all(bf16[512,2,256]{2,1,0:T(2,128)(2,1)S(1)} %copy.91), channel_id=1, replica_groups=mesh['seq'=8,'vocab'=16] {'seq'}, dimensions={0} | all-to-all | bytes 1048576 | tf_op jit(solution)/shard_map/all_to_all | solution.py:76
  358.3 68.5 %all-gather.8.cloned.1.call-done = bf16[1024,2,2048]{2,0,1:T(8,128)(2,1)} async-done(((bf16[64,2,2048]{2,0,1:T(8,128)(2,1)}), bf16[1024,2,2048]{2,0,1:T(8,128)(2,1)}) %all-gather.8.cloned.1.call-update) | async-done | bytes 8388624 | tf_op jit(solution)/shard_map/all_gather | solution.py:80
  426.8 17.6 %fusion.29 = (f32[2,1024]{1,0:T(2,128)S(1)}, f32[1024,2,1024]{2,0,1:T(8,128)}) fusion(f32[1024]{0:T(1024)S(1)} %copy-done.6, pred[1024,2]{0,1:T(4,128)(4,1)S(1)} %broadcast_compare_fusion.1, bf16[1024,2,2048]{2,0,1:T(8,128)(2,1)} %all-gather.8.cloned.1.call-done, bf16[2048,1024]{1,0:T(8,128)(2,1)} %param.15), kind=kOutput, calls=%fused_computation.44 | convolution fusion | flops 8600418304 | bytes 20985856 | tf_op jit(solution)/shard_map/dot_general | solution.py:82
  444.4 14.7 %psum.7 = f32[2,1024]{1,0:T(2,128)S(1)} all-reduce(f32[2,1024]{1,0:T(2,128)S(1)} %get-tuple-element.387), channel_id=1, replica_groups=mesh['seq'=8,'vocab'=16] {'seq'}, use_global_device_ids=true, to_apply=%region_6.7 | all-reduce | flops 2048 | bytes 16384 | tf_op jit(solution)/shard_map/psum | solution.py:98
  459.8 5.2 fusion.40
  465.0 19.0 %convolution_convert_fusion = bf16[1024,2,2048]{2,0,1:T(8,128)(2,1)} fusion(f32[1024,2,1024]{2,0,1:T(8,128)S(1)} %copy-done.1, bf16[2048,1024]{1,0:T(8,128)(2,1)} %param.15, f32[2,1024]{1,0:T(2,128)S(1)} %broadcast_divide_fusion, f32[1024]{0:T(1024)S(1)} %copy-done.6, pred[1024,2]{0,1:T(4,128)(4,1)S(1)} %broadcast_compare_fusion.1, ...), kind=kOutput, calls=%fused_computation.45 | convolution fusion | flops 8623489024 | bytes 22034432 | tf_op jit(solution)/shard_map/dot_general | solution.py:103
  483.9 83.3 %reduce-scatter.2.cloned.1.call-done = bf16[64,2,2048]{2,0,1:T(8,128)(2,1)} async-done(((bf16[1024,2,2048]{2,0,1:T(8,128)(2,1)}), bf16[64,2,2048]{2,0,1:T(8,128)(2,1)}) %reduce-scatter.2.cloned.1.call-update) | async-done | bytes 524304 | tf_op jit(solution)/shard_map/reduce_scatter | solution.py:109
  (275 shorter events, 127.4 us)
Async XLA Ops:
  7.2 39.4 %copy-start.3 = (bf16[64,2,2048]{2,1,0:T(2,128)(2,1)S(1)}, bf16[64,2,2048]{2,1,0:T(2,128)(2,1)}, u32[]{:S(2)}) copy-start(bf16[64,2,2048]{2,1,0:T(2,128)(2,1)} %param.10) | copy-start | bytes 1572868
  7.2 92.1 %all-gather.6.cloned.1.call-start = ((), (), s32[]{:S(2)}) async-start(), calls=%async_computation.6 | async-start | bytes 8912896 | tf_op jit(solution)/shard_map/all_gather | solution.py:64
  27.9 144.8 %copy-start.4 = (s32[2]{0:T(128)S(1)}, s32[2]{0:T(128)}, u32[]{:S(2)}) copy-start(s32[2]{0:T(128)} %param.17) | copy-start | bytes 28
  27.9 144.8 %all-gather.4.cloned.1.call-start = ((), (), s32[]{:S(2)}) async-start(), calls=%async_computation.5 | async-start | bytes 8912896 | tf_op jit(solution)/shard_map/all_gather | solution.py:63
  49.0 13.7 %all-to-all-start.1 = ((bf16[8,2,16384]{2,1,0:T(2,128)(2,1)}), bf16[8,2,16384]{2,1,0:T(2,128)(2,1)S(1)}, u32[]{:S(2)}, u32[]{:S(2)}) async-start(bf16[8,2,16384]{2,1,0:T(2,128)(2,1)} %reshape.210), calls=%async_computation.1 | async-start | bytes 1048576 | tf_op jit(solution)/shard_map/all_to_all | solution.py:21
  52.5 374.3 %all-gather.8.cloned.1.call-start = ((), (), s32[]{:S(2)}) async-start(), calls=%async_computation.7 | async-start | bytes 8912896 | tf_op jit(solution)/shard_map/all_gather | solution.py:80
  178.7 3.5 copy-start
  189.3 3.5 copy-start
  199.8 3.5 copy-start
  210.3 3.5 copy-start
  220.9 3.5 copy-start
  231.4 3.5 copy-start
  241.9 3.5 copy-start
  252.5 3.5 copy-start
  263.0 3.5 copy-start
  273.5 3.5 copy-start
  284.1 3.5 copy-start
  294.6 3.5 copy-start
  305.1 3.5 copy-start
  315.7 3.5 copy-start
  326.2 3.5 copy-start
  336.7 3.5 copy-start
  341.2 15.4 %copy-start.2 = (bf16[64,2,2048]{2,1,0:T(2,128)(2,1)S(1)}, bf16[64,2,2048]{2,1,0:T(2,128)(2,1)}, u32[]{:S(2)}) copy-start(bf16[64,2,2048]{2,1,0:T(2,128)(2,1)} %param.13) | copy-start | bytes 1572868
  341.2 15.7 %copy-start.5 = (f32[2048]{0:T(1024)S(1)}, f32[2048]{0:T(1024)}, u32[]{:S(2)}) copy-start(f32[2048]{0:T(1024)} %param.14) | copy-start | bytes 24580
  341.2 85.6 %copy-start.6 = (f32[1024]{0:T(1024)S(1)}, f32[1024]{0:T(1024)}, u32[]{:S(2)}) copy-start(f32[1024]{0:T(1024)} %param.16) | copy-start | bytes 12292
  358.0 209.2 %reduce-scatter.2.cloned.1.call-start = ((), (), s32[]{:S(2)}) async-start(), calls=%async_computation.8 | async-start | bytes 8912896 | tf_op jit(solution)/shard_map/reduce_scatter | solution.py:109
  459.1 5.9 %copy-start.1 = (f32[1024,2,1024]{2,0,1:T(8,128)S(1)}, f32[1024,2,1024]{2,0,1:T(8,128)}, u32[]{:S(2)}) copy-start(f32[1024,2,1024]{2,0,1:T(8,128)} %get-tuple-element.388) | copy-start | bytes 25165828
Sparse Core Ops, SparseCore 0:
  28.0 71.2 all-gather.5
  102.1 70.5 all-gather.3
  358.1 68.6 all-gather.7
  484.0 83.1 reduce-scatter.1
where the time goes:
time: 577 us; the launch traced here: 576 us
  waiting for transfers between devices  270 us (47%)
  matrix products  140 us (24%)
  blocking collectives  56.6 us (10%)
  local copies, waits for them, and re-layouts  55.2 us (10%)
  other arithmetic  34.8 us (6%)
  between operations  14 us (2%)
    reduce_scatter x1, waiting for transfers between devices, local(): lax.psum_scatter(flattened.reshape(gathered_rows, docs_count, head_weight...  83.3 us
    all_gather x1, waiting for transfers between devices, local(): key_piece = lax.all_gather(key_heads, 'vocab', axis=0, tiled=True)  73.3 us
    all_gather x1, waiting for transfers between devices, local(): arrived = lax.all_gather(hidden, 'vocab', axis=0, tiled=True)  68.5 us
    dot_general x16, matrix products, attend_block(): jnp.einsum('bhqk,kbhe->qbhe', weights.astype(jnp.bfloat16), value_split,...  55.5 us
    dot_general x16, matrix products, attend_block(): jnp.einsum('qbhe,kbhe->bhqk', query_split, key_split, preferred_element_t...  48.2 us
    dynamic_slice x64, local copies, waits for them, and re-layouts, local(): lax.scan(attend_block, carry, (key_blocks, value_blocks, shards))  36.4 us
    all_gather x1, waiting for transfers between devices, local(): value_piece = lax.all_gather(value_heads, 'vocab', axis=0, tiled=True)  35 us
    dot_general x1, matrix products, local(): lax.dot_general(dlogits.reshape(gathered_rows * docs_count, dlogits.shape...  19 us
  transfers between devices with their start and end apart: 5, of which 5 were waited for; matrix products, arithmetic and copies ran while one was open for 2% of the time, Pallas kernels for 0%

commit v1 on v0

--- a/solution.py
+++ b/solution.py
@@ -77,7 +77,9 @@
     combined = residual.astype(jnp.float32) + returned.astype(jnp.float32)
     inv_rms = lax.rsqrt(jnp.mean(combined * combined, axis=2, keepdims=True) + epsilon)
     hidden = (combined * inv_rms * norm_gain).astype(jnp.bfloat16)
-    arrived = lax.all_gather(hidden, "vocab", axis=0, tiled=True)
+    arrived = jnp.concatenate(
+        lax.all_to_all(jnp.stack([hidden] * lax.axis_size("vocab")), "vocab", 0, 0), axis=0
+    )
     row_count = arrived.shape[0]
     flattened = jnp.dot(
         arrived.reshape(row_count * docs_count, arrived.shape[2]),

time: 577 us -> 671 us (1.16)
  waiting for transfers between devices: 270 us -> 349 us
  local copies, waits for them, and re-layouts: 55.2 us -> 67.7 us
    all_to_all x0 -> x1, waiting for transfers between devices: none -> 143 us  [local(): lax.all_to_all(jnp.stack([hidden] * lax.axis_size('vocab')), 'vocab', 0, 0)]
    all_gather x1 -> x0, waiting for transfers between devices: 68.5 us -> none  [local(): arrived = lax.all_gather(hidden, 'vocab', axis=0, tiled=True)]
    all_to_all x0 -> x1, local copies, waits for them, and re-layouts: none -> 8.25 us  [local(): lax.all_to_all(jnp.stack([hidden] * lax.axis_size('vocab')), 'vocab', 0, 0)]
  transfers between devices with their start and end apart: 5 -> 5, of which waited for: 5 -> 5; matrix products, arithmetic and copies ran while one was open for 2% -> 1% of each run, Pallas kernels for 0% -> 0%
where the time goes in v1:
time: 671 us; the launch traced here: 670 us
  waiting for transfers between devices  349 us (52%)
  matrix products  140 us (21%)
  local copies, waits for them, and re-layouts  67.7 us (10%)
  blocking collectives  55.4 us (8%)
  other arithmetic  34 us (5%)
  between operations  14 us (2%)
  starting transfers between devices  9.1 us (1%)
    all_to_all x1, waiting for transfers between devices, local(): lax.all_to_all(jnp.stack([hidden] * lax.axis_size('vocab')), 'vocab', 0, 0)  143 us
    reduce_scatter x1, waiting for transfers between devices, local(): lax.psum_scatter(flattened.reshape(gathered_rows, docs_count, head_weight...  87.4 us
    all_gather x1, waiting for transfers between devices, local(): key_piece = lax.all_gather(key_heads, 'vocab', axis=0, tiled=True)  73.3 us
    dot_general x16, matrix products, attend_block(): jnp.einsum('bhqk,kbhe->qbhe', weights.astype(jnp.bfloat16), value_split,...  55.5 us
    dot_general x16, matrix products, attend_block(): jnp.einsum('qbhe,kbhe->bhqk', query_split, key_split, preferred_element_t...  48 us
    dynamic_slice x64, local copies, waits for them, and re-layouts, local(): lax.scan(attend_block, carry, (key_blocks, value_blocks, shards))  36.4 us
    all_gather x1, waiting for transfers between devices, local(): value_piece = lax.all_gather(value_heads, 'vocab', axis=0, tiled=True)  35 us
    dot_general x1, matrix products, local(): lax.dot_general(dlogits.reshape(gathered_rows * docs_count, dlogits.shape...  18.9 us
  transfers between devices with their start and end apart: 5, of which 5 were waited for; matrix products, arithmetic and copies ran while one was open for 1% of the time, Pallas kernels for 0%

profile of v1, /device:TPU:0, one launch (start us, length us, event | category | flops | bytes accessed | tf_op | source)
XLA Modules:
  0.0 670.1 jit_solution(5804131400767512240)
XLA Ops:
  10.6 14.7 %all_to_all.65 = bf16[8,2,16384]{2,1,0:T(2,128)(2,1)S(1)} all-to-all(bf16[8,2,16384]{2,1,0:T(2,128)(2,1)S(1)} %reshape.213), channel_id=1, replica_groups=mesh['seq'=8,'vocab'=16] {'seq'}, dimensions={0} | all-to-all | bytes 1048576 | tf_op jit(solution)/shard_map/all_to_all | solution.py:23
  31.2 12.8 %all_to_all.66 = bf16[8,2,16384]{2,1,0:T(2,128)(2,1)S(1)} all-to-all(bf16[8,2,16384]{2,1,0:T(2,128)(2,1)S(1)} %reshape.209), channel_id=1, replica_groups=mesh['seq'=8,'vocab'=16] {'seq'}, dimensions={0} | all-to-all | bytes 1048576 | tf_op jit(solution)/shard_map/all_to_all | solution.py:22
  49.0 3.5 all-to-all-start.1
  52.5 10.2 %all-to-all-done.1 = bf16[8,2,16384]{2,1,0:T(2,128)(2,1)S(1)} async-done(((bf16[8,2,16384]{2,1,0:T(2,128)(2,1)}), bf16[8,2,16384]{2,1,0:T(2,128)(2,1)S(1)}, u32[]{:S(2)}, u32[]{:S(2)}) %all-to-all-start.1) | async-done | bytes 524320 | tf_op jit(solution)/shard_map/all_to_all | solution.py:21
  64.3 35.0 %all-gather.5.cloned.1.call-done = bf16[8192,2,256]{2,0,1:T(8,128)(2,1)} async-done(((bf16[512,2,256]{2,0,1:T(8,128)(2,1)}), bf16[8192,2,256]{2,0,1:T(8,128)(2,1)}) %all-gather.5.cloned.1.call-update) | async-done | bytes 8388624 | tf_op jit(solution)/shard_map/all_gather | solution.py:64
  99.3 73.3 %all-gather.3.cloned.1.call-done = bf16[8192,2,256]{2,0,1:T(8,128)(2,1)} async-done(((bf16[512,2,256]{2,0,1:T(8,128)(2,1)}), bf16[8192,2,256]{2,0,1:T(8,128)(2,1)}) %all-gather.3.cloned.1.call-update) | async-done | bytes 8388624 | tf_op jit(solution)/shard_map/all_gather | solution.py:63
  172.6 168.3 %while.20 = (s32[]{:T(128)}, f32[2,2,512]{2,1,0:T(2,128)S(1)}, f32[2,2,512]{2,1,0:T(2,128)S(1)}, f32[512,2,2,128]{0,3,2,1:T(8,128)S(1)}, s32[16]{0:T(128)S(1)}, ...) while((s32[]{:T(128)}, f32[2,2,512]{2,1,0:T(2,128)S(1)}, ...), condition=%wide.region_3.4_spmd.clone.clone, body=%wide.region_0.3_spmd.clone.clone.sunk | while | flops 549213184 | bytes 37364912 | solution.py:69
  178.7 3.5 fusion.75
  189.2 3.5 fusion.75
  199.7 3.5 fusion.75
  210.2 3.5 fusion.75
  220.8 3.5 fusion.75
  231.3 3.5 fusion.75
  241.8 3.5 fusion.75
  252.3 3.5 fusion.75
  262.8 3.5 fusion.75
  273.3 3.5 fusion.75
  283.9 3.5 fusion.75
  294.4 3.5 fusion.75
  315.4 3.5 fusion.75
  325.9 3.5 fusion.75
  336.5 3.5 fusion.75
  341.5 14.5 %all_to_all.67 = bf16[512,2,256]{2,1,0:T(2,128)(2,1)S(1)} all-to-all(bf16[512,2,256]{2,1,0:T(2,128)(2,1)S(1)} %copy.93), channel_id=1, replica_groups=mesh['seq'=8,'vocab'=16] {'seq'}, dimensions={0} | all-to-all | bytes 1048576 | tf_op jit(solution)/shard_map/all_to_all | solution.py:76
  356.9 4.3 stack.2
  361.2 5.3 all-to-all-start.4
  366.8 143.0 %all-to-all-done.4 = bf16[16,64,2,2048]{3,1,2,0:T(8,128)(2,1)} async-done(((bf16[16,64,2,2048]{3,1,2,0:T(8,128)(2,1)}), bf16[16,64,2,2048]{3,1,2,0:T(8,128)(2,1)}, u32[]{:S(2)}, u32[]{:S(2)}) %all-to-all-start.4) | async-done | bytes 8388640 | tf_op jit(solution)/shard_map/all_to_all | solution.py:81
  509.8 8.3 %copy.85 = bf16[16,64,2,2048]{3,1,0,2:T(8,128)(2,1)} copy(bf16[16,64,2,2048]{3,1,2,0:T(8,128)(2,1)} %all-to-all-done.4) | data formatting | bytes 16777216 | tf_op jit(solution)/shard_map/all_to_all | solution.py:81
  518.0 17.6 %fusion.29 = (f32[2,1024]{1,0:T(2,128)S(1)}, f32[1024,2,1024]{2,0,1:T(8,128)}) fusion(f32[1024]{0:T(1024)S(1)} %copy-done.6, pred[1024,2]{0,1:T(4,128)(4,1)S(1)} %broadcast_compare_fusion.1, bf16[1024,2,2048]{2,0,1:T(8,128)(2,1)} %bitcast.86, bf16[2048,1024]{1,0:T(8,128)(2,1)} %param.15), kind=kOutput, calls=%fused_computation.44 | convolution fusion | flops 8600418304 | bytes 20985856 | tf_op jit(solution)/shard_map/dot_general | solution.py:84
  535.6 13.4 %psum.7 = f32[2,1024]{1,0:T(2,128)S(1)} all-reduce(f32[2,1024]{1,0:T(2,128)S(1)} %get-tuple-element.387), channel_id=1, replica_groups=mesh['seq'=8,'vocab'=16] {'seq'}, use_global_device_ids=true, to_apply=%region_6.7 | all-reduce | flops 2048 | bytes 16384 | tf_op jit(solution)/shard_map/psum | solution.py:100
  549.7 5.2 fusion.40
  554.9 18.9 %convolution_convert_fusion = bf16[1024,2,2048]{2,0,1:T(8,128)(2,1)} fusion(f32[1024,2,1024]{2,0,1:T(8,128)S(1)} %copy-done.1, bf16[2048,1024]{1,0:T(8,128)(2,1)} %param.15, f32[2,1024]{1,0:T(2,128)S(1)} %broadcast_divide_fusion, f32[1024]{0:T(1024)S(1)} %copy-done.6, pred[1024,2]{0,1:T(4,128)(4,1)S(1)} %broadcast_compare_fusion.1, ...), kind=kOutput, calls=%fused_computation.45 | convolution fusion | flops 8623489024 | bytes 22034432 | tf_op jit(solution)/shard_map/dot_general | solution.py:105
  573.9 87.4 %reduce-scatter.2.cloned.1.call-done = bf16[64,2,2048]{2,0,1:T(8,128)(2,1)} async-done(((bf16[1024,2,2048]{2,0,1:T(8,128)(2,1)}), bf16[64,2,2048]{2,0,1:T(8,128)(2,1)}) %reduce-scatter.2.cloned.1.call-update) | async-done | bytes 524304 | tf_op jit(solution)/shard_map/reduce_scatter | solution.py:111
  (276 shorter events, 135.8 us)
Async XLA Ops:
  7.2 39.4 %copy-start.3 = (bf16[64,2,2048]{2,1,0:T(2,128)(2,1)S(1)}, bf16[64,2,2048]{2,1,0:T(2,128)(2,1)}, u32[]{:S(2)}) copy-start(bf16[64,2,2048]{2,1,0:T(2,128)(2,1)} %param.10) | copy-start | bytes 1572868
  7.2 92.1 %all-gather.5.cloned.1.call-start = ((), (), s32[]{:S(2)}) async-start(), calls=%async_computation.7 | async-start | bytes 8912896 | tf_op jit(solution)/shard_map/all_gather | solution.py:64
  27.8 144.8 %copy-start.4 = (s32[2]{0:T(128)S(1)}, s32[2]{0:T(128)}, u32[]{:S(2)}) copy-start(s32[2]{0:T(128)} %param.17) | copy-start | bytes 28
  27.9 144.8 %all-gather.3.cloned.1.call-start = ((), (), s32[]{:S(2)}) async-start(), calls=%async_computation.6 | async-start | bytes 8912896 | tf_op jit(solution)/shard_map/all_gather | solution.py:63
  49.0 13.7 %all-to-all-start.1 = ((bf16[8,2,16384]{2,1,0:T(2,128)(2,1)}), bf16[8,2,16384]{2,1,0:T(2,128)(2,1)S(1)}, u32[]{:S(2)}, u32[]{:S(2)}) async-start(bf16[8,2,16384]{2,1,0:T(2,128)(2,1)} %reshape.211), calls=%async_computation.1 | async-start | bytes 1048576 | tf_op jit(solution)/shard_map/all_to_all | solution.py:21
  178.7 3.5 copy-start
  189.2 3.5 copy-start
  199.7 3.5 copy-start
  210.2 3.5 copy-start
  220.8 3.5 copy-start
  231.3 3.5 copy-start
  241.8 3.5 copy-start
  252.3 3.5 copy-start
  262.8 3.5 copy-start
  273.3 3.5 copy-start
  283.9 3.5 copy-start
  294.4 3.5 copy-start
  304.9 3.5 copy-start
  315.4 3.5 copy-start
  325.9 3.5 copy-start
  336.4 3.5 copy-start
  340.9 15.4 %copy-start.2 = (bf16[64,2,2048]{2,1,0:T(2,128)(2,1)S(1)}, bf16[64,2,2048]{2,1,0:T(2,128)(2,1)}, u32[]{:S(2)}) copy-start(bf16[64,2,2048]{2,1,0:T(2,128)(2,1)} %param.13) | copy-start | bytes 1572868
  340.9 15.7 %copy-start.5 = (f32[2048]{0:T(1024)S(1)}, f32[2048]{0:T(1024)}, u32[]{:S(2)}) copy-start(f32[2048]{0:T(1024)} %param.14) | copy-start | bytes 24580
  361.2 148.6 %all-to-all-start.4 = ((bf16[16,64,2,2048]{3,1,2,0:T(8,128)(2,1)}), bf16[16,64,2,2048]{3,1,2,0:T(8,128)(2,1)}, u32[]{:S(2)}, u32[]{:S(2)}) async-start(bf16[16,64,2,2048]{3,1,2,0:T(8,128)(2,1)} %stack.2), calls=%async_computation.4 | async-start | bytes 16777216 | tf_op jit(solution)/shard_map/all_to_all | solution.py:81
  366.5 294.8 %reduce-scatter.2.cloned.1.call-start = ((), (), s32[]{:S(2)}) async-start(), calls=%async_computation.8 | async-start | bytes 8912896 | tf_op jit(solution)/shard_map/reduce_scatter | solution.py:111
  366.8 151.2 %copy-start.6 = (f32[1024]{0:T(1024)S(1)}, f32[1024]{0:T(1024)}, u32[]{:S(2)}) copy-start(f32[1024]{0:T(1024)} %param.16) | copy-start | bytes 12292
  549.0 5.9 copy-start.1
Sparse Core Ops, SparseCore 0:
  28.0 71.2 all-gather.4
  102.1 70.5 all-gather.2
  574.0 87.1 reduce-scatter.1
